TPU v7x, 32 devices: a whole 2x2x4 slice. The times are simulated.
32 devices in a mesh: gx: 4 (over y, x), gy: 2 (over core), gz: 4 (over z).
Axes of the slice: x: 2, y: 2, z: 4, core: 2. Of those that a mesh axis runs over, the one named last changes fastest.
Arguments:
- fields: float32 [64, 8, 16, 256], P(('gx', 'gy', 'gz')), may hold values from 0 to 1
- seed_labels: int32 [64, 256], P(('gx', 'gy', 'gz')), may hold values from 0 to 3
- coords: int32 [48, 3], replicated, may hold values from 0 to 5, as said below
- neighbours: int32 [48, 6], replicated, may hold values from -1 to 47, as said below
- owner_before: int32 [48], replicated, may hold values from 0 to 63, as said below
- owner_after: int32 [48], replicated, may hold values from 0 to 63, as said below
- couple: float32 [4, 4], replicated, may hold values from -3 to 3
- latent: float32 [4, 4], replicated, may hold values from -3 to 3
- diffuse: float32 [4], replicated, may hold values from 0.3 to 1.5
- thermal_gain: float32 [4], replicated, may hold values from -4 to 4
Outputs:
- fields_out: float32 [64, 8, 16, 256], P(('gx', 'gy', 'gz'))
Inputs may be any that keep to these rules, and one draw needn't show every extreme that they name: `coords`: a permutation of the positions of a 4 x 2 x 6 grid of blocks. `neighbours`: the block beside b across each side by coords; -1 beyond the ends along x and y; along z the blocks close into a loop. `owner_before`: distinct for distinct blocks; a place p is slot p % 2 of device p // 2, devices counted over gx, gy, gz in order; block b's device has index coords[b, 0] along gx and coords[b, 1] along gy. `owner_after`: distinct for distinct blocks; a block's device after migration is its device before or the next one along gz, cyclic, with the same gx and gy indices; at most one block of a device moves; in every group of devices along gz at least one block moves.
All inputs are finite; a program needn't handle non-finite values.
Results may differ from a plain program's by a relative error of at most 0.0003.
Values sent between devices are 32-bit elements; how exact they have to be, the bound alone decides.
A program may use at most 64 MiB of HBM per device.

v0:
```python
import functools

import jax
import jax.numpy as jnp
from jax import lax
from jax.experimental import pallas as pl
from jax.experimental.pallas import tpu as pltpu
from jax.sharding import PartitionSpec as P

NPHASE = 4
STEPS = 2
LANES = 128
SEED_GAIN = 2.0
MESH = pl.DeviceIdType.MESH


def kernel(
    sizes,
    fields,
    seeds,
    coords,
    before,
    after,
    couple,
    latent,
    diffuse,
    gain,
    out,
    recv,
    seed_recv,
    vals,
    xsend,
    xghost,
    ysend,
    yghost,
    result,
    outbuf,
    in_send,
    in_recv,
    seed_send,
    seed_got,
    x_send,
    x_recv,
    y_send,
    y_recv,
    out_send,
    out_recv,
    local_sem,
):
    gx_n, gy_n, gz_n, nblk, cells, surface = sizes
    slots, nfield = outbuf.shape[1], outbuf.shape[2]
    rows = outbuf.shape[3]
    halves = surface // LANES
    per_column = vals.shape[1]
    x_parts = gz_n // halves
    gx, gy, gz = lax.axis_index("gx"), lax.axis_index("gy"), lax.axis_index("gz")
    odd_x, odd_y = gx % 2, gy % 2

    def part_of(g):
        a, b = g // halves, g % halves
        xh = a + odd_x * (x_parts - 1 - 2 * a)
        yh = b + odd_y * (halves - 1 - 2 * b)
        return xh, yh

    def window(ref, g):
        xh, yh = part_of(g)
        x0 = pl.multiple_of(xh * rows, rows)
        y0 = pl.multiple_of(yh * LANES, LANES)
        return ref.at[:, :, pl.ds(x0, rows), pl.ds(y0, LANES)]

    def seed_window(g):
        _, yh = part_of(g)
        return seeds.at[:, pl.ds(pl.multiple_of(yh * LANES, LANES), LANES)]

    xh, yh = part_of(gz)
    xpos = gx * x_parts + xh
    ypos = gy * halves + yh
    x_total, y_total = gx_n * x_parts, gy_n * halves
    dir_x = 1 - 2 * odd_x
    dir_y = 1 - 2 * odd_y
    xlo_in, xhi_in = xh > 0, xh < x_parts - 1
    ylo_in, yhi_in = yh > 0, yh < halves - 1
    sides = []
    for exists, inside, step_x, step_y, move in (
        (xpos > 0, xlo_in, -1, 0, -halves * dir_x),
        (xpos < x_total - 1, xhi_in, 1, 0, halves * dir_x),
        (ypos > 0, ylo_in, 0, -1, -dir_y),
        (ypos < y_total - 1, yhi_in, 0, 1, dir_y),
    ):
        ins = inside.astype(jnp.int32)
        device = (gx + step_x * (1 - ins), gy + step_y * (1 - ins), gz + move * ins)
        sides.append((exists, inside, device))

    barrier = pltpu.get_barrier_semaphore()
    for d in range(1, gz_n):
        pl.semaphore_signal(
            barrier, inc=1, device_id=(gx, gy, (gz + d) % gz_n), device_id_type=MESH
        )
    expected = gz_n - 1
    for exists, inside, device in sides:
        outside = jnp.logical_and(exists, jnp.logical_not(inside))

        @pl.when(outside)
        def _(device=device):
            pl.semaphore_signal(barrier, inc=1, device_id=device, device_id_type=MESH)

        expected = expected + outside.astype(jnp.int32)
    pl.semaphore_wait(barrier, expected)

    moves = []
    for d in range(gz_n - 1, 0, -1):
        to = (gz + d) % gz_n
        for src, dst, s_sem, r_sem in (
            (window(fields, to), recv.at[pl.ds(slots * gz, slots)], in_send, in_recv),
            (seed_window(to), seed_recv.at[gz], seed_send, seed_got),
        ):
            copy = pltpu.make_async_remote_copy(
                src_ref=src,
                dst_ref=dst,
                send_sem=s_sem.at[d - 1],
                recv_sem=r_sem.at[d - 1],
                device_id=(gx, gy, to),
                device_id_type=MESH,
            )
            copy.start()
            moves.append(copy)
    own = pltpu.make_async_copy(
        window(fields, gz), recv.at[pl.ds(slots * gz, slots)], local_sem.at[0]
    )
    own.start()
    own_seed = pltpu.make_async_copy(seed_window(gz), seed_recv.at[gz], local_sem.at[1])
    own_seed.start()

    base = (gx * gy_n + gy) * (gz_n * slots)
    places = gz_n * slots

    def lookup(b, carry):
        source, depth = carry
        here = jnp.logical_and(coords[0, b] == gx, coords[1, b] == gy)
        z = jnp.where(here, coords[2, b], -1)
        was = before[b] - base
        now = jnp.where(here, after[b] - base, -1)
        source = tuple(jnp.where(z == k, was, source[k]) for k in range(per_column))
        depth = tuple(jnp.where(now == q, z, depth[q]) for q in range(places))
        return source, depth

    source, depth = lax.fori_loop(
        0,
        nblk,
        lookup,
        ((jnp.int32(0),) * per_column, (jnp.int32(-1),) * places),
    )

    own.wait()
    own_seed.wait()
    for copy in moves:
        copy.wait()

    marks = []
    for k in range(per_column):
        p = source[k]
        vals[:, k] = recv[p]
        pair = seed_recv[p // slots]
        row = pair[0:1]
        for s in range(1, slots):
            row = jnp.where(p % slots == s, pair[s : s + 1], row)
        marks.append(row[None])
    marks = jnp.concatenate(marks, 0)

    shape = (per_column, rows, LANES)
    lane = lax.broadcasted_iota(jnp.int32, shape, 2)
    row_id = lax.broadcasted_iota(jnp.int32, shape, 1)
    z_cell = lane % cells
    group = lane // cells
    xglob = (row_id + (gx * cells + xh * rows)).astype(jnp.float32)

    def rolled(v, shift):
        shift = shift % LANES
        return v if shift == 0 else pltpu.roll(v, shift, 2)

    def exchange(step, old):
        low_y = jnp.zeros(shape, jnp.float32)
        high_y = low_y
        for f in range(nfield):
            v = old[f]
            xsend[step, 0, :, f : f + 1, :] = v[:, 0:1, :]
            xsend[step, 1, :, f : f + 1, :] = v[:, rows - 1 : rows, :]
            low_y = jnp.where(group == f, rolled(v, cells * f), low_y)
            high_y = jnp.where(group == f, rolled(v, cells * f + cells), high_y)
        ysend[step, 0] = low_y
        ysend[step, 1] = high_y
        for phase in ("start", "wait"):
            for side, (exists, _, device) in enumerate(sides):
                send, ghost, s_sem, r_sem = (
                    (xsend, xghost, x_send, x_recv)
                    if side < 2
                    else (ysend, yghost, y_send, y_recv)
                )
                e = side % 2

                @pl.when(exists)
                def _(send=send, ghost=ghost, s_sem=s_sem, r_sem=r_sem, e=e, device=device):
                    if phase == "start":
                        pltpu.make_async_remote_copy(
                            src_ref=send.at[step, e],
                            dst_ref=ghost.at[step, 1 - e],
                            send_sem=s_sem.at[step, e],
                            recv_sem=r_sem.at[step, 1 - e],
                            device_id=device,
                            device_id_type=MESH,
                        ).start()
                    else:
                        pltpu.make_async_remote_copy(
                            src_ref=send.at[step, e],
                            dst_ref=ghost.at[step, e],
                            send_sem=s_sem.at[step, e],
                            recv_sem=r_sem.at[step, e],
                            device_id=device,
                            device_id_type=MESH,
                        ).wait()

                if phase == "start":

                    @pl.when(jnp.logical_not(exists))
                    def _(send=send, ghost=ghost, e=e):
                        ghost[step, e] = send[step, e]

    def laplace(step, f, v):
        below_x = jnp.concatenate([xghost[step, 0, :, f : f + 1, :], v[:, :-1, :]], 1)
        above_x = jnp.concatenate([v[:, 1:, :], xghost[step, 1, :, f : f + 1, :]], 1)
        below_y = jnp.where(
            group == 0, rolled(yghost[step, 0], -cells * f), rolled(v, cells)
        )
        above_y = jnp.where(
            group == LANES // cells - 1,
            rolled(yghost[step, 1], -cells * f - cells),
            rolled(v, -cells),
        )
        before_k = jnp.concatenate([v[-1:], v[:-1]], 0)
        after_k = jnp.concatenate([v[1:], v[:1]], 0)
        below_z = jnp.where(z_cell == 0, rolled(before_k, 1 - cells), rolled(v, 1))
        above_z = jnp.where(z_cell == cells - 1, rolled(after_k, cells - 1), rolled(v, -1))
        return below_x + above_x + below_y + above_y + below_z + above_z - 6.0 * v

    for step in range(STEPS):
        src = vals if step == 0 else result.at[step - 1]
        exchange(step, [src[f] for f in range(nfield)])
        thermal = xglob / (2.0 * cells) - 1.0 - 0.25 * step
        change = []
        for k in range(NPHASE):
            phi = src[k]
            drive = gain[k] * thermal
            for j in range(nfield - NPHASE):
                drive = drive + couple[k, j] * src[NPHASE + j]
            if step == 0:
                drive = drive + SEED_GAIN * (marks == k).astype(jnp.float32)
            delta = 0.12 * laplace(step, k, phi) + phi * (1.0 - phi) * (phi - 0.5 + drive)
            new = phi + delta
            result[step, k] = new
            change.append(new - phi)
        for j in range(nfield - NPHASE):
            mu = src[NPHASE + j]
            new = mu + (0.1 * diffuse[j]) * laplace(step, NPHASE + j, mu)
            for k in range(NPHASE):
                new = new - latent[j, k] * change[k]
            result[step, NPHASE + j] = new

    for q in range(places):
        k = depth[q]
        tile = result[STEPS - 1, :, jnp.maximum(k, 0)]
        outbuf[q // slots, q % slots] = jnp.where(k >= 0, tile, 0.0)
    moves = []
    for d in range(gz_n - 1, 0, -1):
        to = (gz + d) % gz_n
        copy = pltpu.make_async_remote_copy(
            src_ref=outbuf.at[to],
            dst_ref=window(out, gz),
            send_sem=out_send.at[d - 1],
            recv_sem=out_recv.at[d - 1],
            device_id=(gx, gy, to),
            device_id_type=MESH,
        )
        copy.start()
        moves.append(copy)
    own = pltpu.make_async_copy(outbuf.at[gz], window(out, gz), local_sem.at[2])
    own.start()
    own.wait()
    for copy in moves:
        copy.wait()


def solution(mesh):
    gx_n, gy_n, gz_n = mesh.shape["gx"], mesh.shape["gy"], mesh.shape["gz"]

    def per_device(fields, seeds, coords, neighbours, before, after, couple, latent, diffuse, gain):
        slots, nfield, cells, surface = fields.shape
        nblk = coords.shape[0]
        per_column = nblk // (gx_n * gy_n)
        halves = surface // LANES
        rows = cells * halves // gz_n
        f32, i32 = jnp.float32, jnp.int32
        dma = pltpu.SemaphoreType.DMA
        smem = pl.BlockSpec(memory_space=pltpu.SMEM)
        anyspace = pl.BlockSpec(memory_space=pl.ANY)
        faces_x = (STEPS, 2, per_column, nfield, LANES)
        faces_y = (STEPS, 2, per_column, rows, LANES)
        return pl.pallas_call(
            functools.partial(kernel, (gx_n, gy_n, gz_n, nblk, cells, surface)),
            out_shape=jax.ShapeDtypeStruct(fields.shape, f32),
            in_specs=[anyspace, anyspace] + [smem] * 7,
            out_specs=anyspace,
            scratch_shapes=[
                pltpu.VMEM((gz_n * slots, nfield, rows, LANES), f32),
                pltpu.VMEM((gz_n, slots, LANES), i32),
                pltpu.VMEM((nfield, per_column, rows, LANES), f32),
                pltpu.VMEM(faces_x, f32),
                pltpu.VMEM(faces_x, f32),
                pltpu.VMEM(faces_y, f32),
                pltpu.VMEM(faces_y, f32),
                pltpu.VMEM((STEPS, nfield, per_column, rows, LANES), f32),
                pltpu.VMEM((gz_n, slots, nfield, rows, LANES), f32),
                dma((gz_n,)),
                dma((gz_n,)),
                dma((gz_n,)),
                dma((gz_n,)),
                dma((STEPS, 2)),
                dma((STEPS, 2)),
                dma((STEPS, 2)),
                dma((STEPS, 2)),
                dma((gz_n,)),
                dma((gz_n,)),
                dma((3,)),
            ],
            compiler_params=pltpu.CompilerParams(collective_id=0, has_side_effects=True),
        )(fields, seeds, coords.T, before, after, couple, latent, diffuse, gain)

    placed = (
        P(("gx", "gy", "gz"), None, None, None),
        P(("gx", "gy", "gz"), None),
    ) + (P(),) * 8
    return jax.shard_map(
        per_device,
        mesh=mesh,
        in_specs=placed,
        out_specs=P(("gx", "gy", "gz"), None, None, None),
        check_vma=False,
    )
```

profile of v0, /device:TPU:0, one launch (start us, length us, event | category | flops | bytes accessed | tf_op | source)
XLA Modules:
  0.0 28.9 jit_solution(4720446486380928615)
XLA Ops:
  0.0 27.3 %shard_map.91 = f32[2,8,16,256]{3,2,1,0:T(8,128)} custom-call(f32[2,8,16,256]{3,2,1,0:T(8,128)} %fields.1, s32[2,256]{1,0:T(2,128)} %seeds.1, s32[3,48]{1,0:T(4,128)} %bitcast.1, s32[48]{0:T(128)} %before.1, s32[48]{0:T(128)} %after.1, f32[4,4]{1,0:T(4,128)} %couple.1, f32[4,4]{1,0:T(4,128)} %latent.1, f32[4]{0:T(128)} %diffuse.1, f32[4]{0:T(128)} %gain.1), custom_call_target="tpu_custom_call" | custom-call | tf_op jit(solution)/shard_map/pallas_call | solution.py:307
  27.3 1.7 %copy.11 = f32[2,8,16,256]{3,2,1,0:T(8,128)} copy(f32[2,8,16,256]{3,2,1,0:T(8,128)} %shard_map.91) | data formatting | bytes 524288
where the time goes:
time: 29.2 us; the launch traced here: 28.9 us
  Pallas kernels  27.3 us (93%)
  local copies, waits for them, and re-layouts  1.67 us (6%)
    pallas_call x1, Pallas kernels, per_device(): pl.pallas_call(functools.partial(kernel, (gx_n, gy_n, gz_n, nblk, cells,...  27.3 us
    unnamed x1, local copies, waits for them, and re-layouts  1.67 us

commit v1 on v0

--- a/solution.py
+++ b/solution.py
@@ -306,9 +306,9 @@
         faces_y = (STEPS, 2, per_column, rows, LANES)
         return pl.pallas_call(
             functools.partial(kernel, (gx_n, gy_n, gz_n, nblk, cells, surface)),
-            out_shape=jax.ShapeDtypeStruct(fields.shape, f32),
+            out_shape=pltpu.VMEM(fields.shape, f32),
             in_specs=[anyspace, anyspace] + [smem] * 7,
-            out_specs=anyspace,
+            out_specs=pl.BlockSpec(memory_space=pltpu.VMEM),
             scratch_shapes=[
                 pltpu.VMEM((gz_n * slots, nfield, rows, LANES), f32),
                 pltpu.VMEM((gz_n, slots, LANES), i32),

time: 29.2 us -> 28 us (0.959)
  local copies, waits for them, and re-layouts: 1.67 us -> 0.71 us
    unnamed x1, local copies, waits for them, and re-layouts: 1.67 us -> 0.71 us
where the time goes in v1:
time: 28 us; the launch traced here: 27.9 us
  Pallas kernels  27.2 us (97%)
  local copies, waits for them, and re-layouts  0.71 us (3%)
    pallas_call x1, Pallas kernels, per_device(): pl.pallas_call(functools.partial(kernel, (gx_n, gy_n, gz_n, nblk, cells,...  27.2 us
    unnamed x1, local copies, waits for them, and re-layouts  0.71 us

profile of v1, /device:TPU:0, one launch (start us, length us, event | category | flops | bytes accessed | tf_op | source)
XLA Modules:
  0.0 27.9 jit_solution(13388832525851406131)
XLA Ops:
  0.0 27.2 %shard_map.91 = f32[2,8,16,256]{3,2,1,0:T(8,128)S(1)} custom-call(f32[2,8,16,256]{3,2,1,0:T(8,128)} %fields.1, s32[2,256]{1,0:T(2,128)} %seeds.1, s32[3,48]{1,0:T(4,128)} %bitcast.1, s32[48]{0:T(128)} %before.1, s32[48]{0:T(128)} %after.1, f32[4,4]{1,0:T(4,128)} %couple.1, f32[4,4]{1,0:T(4,128)} %latent.1, f32[4]{0:T(128)} %diffuse.1, f32[4]{0:T(128)} %gain.1), custom_call_target="tpu_custom_call" | custom-call | tf_op jit(solution)/shard_map/pallas_call | solution.py:307
  27.2 0.7 %copy.11 = f32[2,8,16,256]{3,2,1,0:T(8,128)} copy(f32[2,8,16,256]{3,2,1,0:T(8,128)S(1)} %shard_map.91) | data formatting | bytes 524288

commit v2 on v1

--- a/solution.py
+++ b/solution.py
@@ -14,7 +14,7 @@
 MESH = pl.DeviceIdType.MESH
 
 
-def kernel(
+def tile_kernel(
     sizes,
     fields,
     seeds,
@@ -289,8 +289,530 @@
         copy.wait()
 
 
+def deep_kernel(sizes, fields, seeds, *refs):
+    gx_n, gy_n, gz_n, nblk, cells, surface = sizes
+    tables, (
+        out,
+        coords,
+        before,
+        after,
+        couple,
+        latent,
+        diffuse,
+        gain,
+        table_sem,
+        mine,
+        bulk,
+        seed_recv,
+        strip,
+        vals,
+        edge,
+        mid,
+        mid_edge,
+        marks,
+        edge_marks,
+        xsend,
+        xghost,
+        xsmall,
+        xgsmall,
+        packed,
+        unpack,
+        result,
+        outbuf,
+        outrecv,
+        local_sem,
+        in_sem,
+        seed_sem,
+        strip_sem,
+        strip_seed_sem,
+        x_sem,
+        xs_sem,
+        out_sem,
+        *arrivals,
+    ) = refs[:7], refs[7:]
+    slots, nfield = mine.shape[0], mine.shape[1]
+    tiles = surface // LANES
+    strip_recv, strip_seed, recv = arrivals[:2], arrivals[2:4], arrivals[4:]
+    per_column = vals.shape[2]
+    rows, halo = cells // gz_n, STEPS
+    ext = rows + 2 * halo
+    strip_lanes = halo * cells
+    per_pack = LANES // strip_lanes
+    packs = -(-nfield // per_pack)
+    places = gz_n * slots
+    gx, gy, gz = lax.axis_index("gx"), lax.axis_index("gy"), lax.axis_index("gz")
+    odd_x = gx % 2
+    turn = 1 - 2 * odd_x
+
+    def tile_of(g):
+        return g + odd_x * (gz_n - 1 - 2 * g)
+
+    part = tile_of(gz)
+    xpos = gx * gz_n + part
+    sides_x = []
+    for exists, inside, step_x in (
+        (xpos > 0, part > 0, -1),
+        (xpos < gx_n * gz_n - 1, part < gz_n - 1, 1),
+    ):
+        ins = inside.astype(jnp.int32)
+        device = (gx + step_x * (1 - ins), gy, gz + step_x * turn * ins)
+        sides_x.append((exists, inside, device))
+    sides_y = ((gy > 0, gy - 1), (gy < gy_n - 1, gy + 1))
+
+    barrier = pltpu.get_barrier_semaphore()
+    expected = gz_n - 1
+    for d in range(1, gz_n):
+        pl.semaphore_signal(
+            barrier, inc=1, device_id=(gx, gy, (gz + d) % gz_n), device_id_type=MESH
+        )
+    for exists, other in sides_y:
+
+        @pl.when(exists)
+        def _(other=other):
+            for z in range(gz_n):
+                pl.semaphore_signal(
+                    barrier, inc=1, device_id=(gx, other, z), device_id_type=MESH
+                )
+
+        expected = expected + gz_n * exists.astype(jnp.int32)
+    for exists, inside, device in sides_x:
+        outside = jnp.logical_and(exists, jnp.logical_not(inside))
+
+        @pl.when(outside)
+        def _(device=device):
+            pl.semaphore_signal(barrier, inc=1, device_id=device, device_id_type=MESH)
+
+        expected = expected + outside.astype(jnp.int32)
+
+    load = pltpu.make_async_copy(fields, mine, local_sem.at[0])
+    load.start()
+    load_seed = pltpu.make_async_copy(seeds, seed_recv.at[gz], local_sem.at[1])
+    load_seed.start()
+    small = (coords, before, after, couple, latent, diffuse, gain)
+    fetches = [
+        pltpu.make_async_copy(src, dst, table_sem.at[n])
+        for n, (src, dst) in enumerate(zip(tables, small))
+    ]
+    for fetch in fetches:
+        fetch.start()
+
+    lane = lax.broadcasted_iota(jnp.int32, (1, 1, LANES), 2)
+
+    def rolled(v, shift):
+        shift = shift % LANES
+        return v if shift == 0 else pltpu.roll(v, shift, 2)
+
+    def pack(s, n, t, e):
+        row = None
+        for j in range(min(per_pack, nfield - n * per_pack)):
+            v = mine[s, pl.ds(n * per_pack + j, 1), :, pl.ds(t * LANES, LANES)]
+            v = rolled(v, strip_lanes * (j + e))
+            row = v if row is None else jnp.where(lane // strip_lanes == j, v, row)
+        return [row[:, q * rows : (q + 1) * rows] for q in range(gz_n)]
+
+    load.wait()
+    for s in range(slots):
+        for n in range(packs):
+            for e, t in ((0, 0), (1, tiles - 1)):
+                for q, row in enumerate(pack(s, n, t, e)):
+                    strip[e, q, s, pl.ds(n, 1)] = row
+            for t in range(tiles - 1):
+                for q, row in enumerate(pack(s, n, t + 1, 0)):
+                    bulk[t, q, s, pl.ds(nfield + n, 1)] = row
+    for t in range(tiles):
+        for q in range(gz_n):
+            bulk[t, q, :, pl.ds(0, nfield)] = mine[
+                :, :, q * rows : (q + 1) * rows, t * LANES : (t + 1) * LANES
+            ]
+    pl.semaphore_wait(barrier, expected)
+
+    for e, (exists, other) in enumerate(sides_y):
+
+        @pl.when(exists)
+        def _(e=e, other=other):
+            for z in range(gz_n):
+                pltpu.make_async_remote_copy(
+                    src_ref=strip.at[e, tile_of(z)],
+                    dst_ref=strip_recv[1 - e].at[pl.ds(slots * gz, slots)],
+                    send_sem=strip_sem.at[e],
+                    recv_sem=strip_sem.at[2 + 1 - e],
+                    device_id=(gx, other, z),
+                    device_id_type=MESH,
+                ).start()
+                pltpu.make_async_remote_copy(
+                    src_ref=seeds,
+                    dst_ref=strip_seed[1 - e].at[gz],
+                    send_sem=strip_seed_sem.at[e],
+                    recv_sem=strip_seed_sem.at[2 + 1 - e],
+                    device_id=(gx, other, z),
+                    device_id_type=MESH,
+                ).start()
+
+    for d in range(1, gz_n):
+        pltpu.make_async_remote_copy(
+            src_ref=seeds,
+            dst_ref=seed_recv.at[gz],
+            send_sem=seed_sem.at[0],
+            recv_sem=seed_sem.at[1],
+            device_id=(gx, gy, (gz + d) % gz_n),
+            device_id_type=MESH,
+        ).start()
+
+    width = [nfield + packs] * (tiles - 1) + [nfield]
+    for t in range(tiles):
+        for d in range(gz_n - 1, 0, -1):
+            to = (gz + d) % gz_n
+            pltpu.make_async_remote_copy(
+                src_ref=bulk.at[t, tile_of(to), :, pl.ds(0, width[t])],
+                dst_ref=recv[t].at[pl.ds(slots * gz, slots), pl.ds(0, width[t])],
+                send_sem=in_sem.at[t],
+                recv_sem=in_sem.at[tiles + t],
+                device_id=(gx, gy, to),
+                device_id_type=MESH,
+            ).start()
+    for t in range(tiles):
+        recv[t][pl.ds(slots * gz, slots), pl.ds(0, width[t])] = bulk[t, part, :, pl.ds(0, width[t])]
+    for fetch in fetches:
+        fetch.wait()
+
+    base = (gx * gy_n + gy) * places
+
+    def lookup(b, carry):
+        source, low, high, depth = carry
+        cy, z = coords[1, b], coords[2, b]
+        same = coords[0, b] == gx
+        was, now = before[b] - base, after[b] - base
+        here = jnp.where(jnp.logical_and(same, cy == gy), z, -1)
+        under = jnp.where(jnp.logical_and(same, cy == gy - 1), z, -1)
+        over = jnp.where(jnp.logical_and(same, cy == gy + 1), z, -1)
+        now = jnp.where(here >= 0, now, -1)
+        source = tuple(jnp.where(here == k, was, source[k]) for k in range(per_column))
+        low = tuple(jnp.where(under == k, was + places, low[k]) for k in range(per_column))
+        high = tuple(jnp.where(over == k, was - places, high[k]) for k in range(per_column))
+        depth = tuple(jnp.where(now == p, z, depth[p]) for p in range(places))
+        return source, low, high, depth
+
+    none = (jnp.int32(0),) * per_column
+    source, low, high, depth = lax.fori_loop(
+        0, nblk, lookup, (none, none, none, (jnp.int32(-1),) * places)
+    )
+
+    def drain(ref, sem):
+        pltpu.make_async_copy(ref, ref, sem).wait()
+
+    def seed_row(ref, p):
+        pair = ref[p // slots]
+        row = pair[0:1]
+        for s in range(1, slots):
+            row = jnp.where(p % slots == s, pair[s : s + 1], row)
+        return row.astype(jnp.float32)
+
+    load_seed.wait()
+    drain(seed_recv.at[pl.ds(0, gz_n - 1)], seed_sem.at[1])
+    for k in range(per_column):
+        row = seed_row(seed_recv, source[k])
+        for t in range(tiles):
+            piece = row[:, t * LANES : (t + 1) * LANES]
+            wide = jnp.broadcast_to(piece, (ext, LANES))
+            marks[t, k] = wide
+            if t > 0:
+                edge_marks[t, k] = wide
+            for x in range(2):
+                xsmall[t, x, k, pl.ds(2 * packs, 1)] = piece
+                if t > 0:
+                    xsmall[t, x, k, pl.ds(0, packs)] = jnp.zeros((packs, LANES), jnp.float32)
+
+    for e, (exists, _) in enumerate(sides_y):
+        spot, at = (0, 0) if e == 0 else (tiles, tiles - 1)
+
+        @pl.when(exists)
+        def _(e=e, spot=spot, at=at):
+            drain(strip_recv[e], strip_sem.at[2 + e])
+            drain(strip_seed[e], strip_seed_sem.at[2 + e])
+            for k in range(per_column):
+                p = (low, high)[e][k]
+                piece = strip_recv[e][p]
+                packed[spot, k] = piece
+                for x, r in ((0, 0), (1, rows - 1)):
+                    for n in range(packs):
+                        xsmall[at, x, k, pl.ds(e * packs + n, 1)] = piece[n, r : r + 1]
+                row = seed_row(strip_seed[e], p)
+                piece = row[:, surface - LANES :] if e == 0 else row[:, :LANES]
+                edge_marks[spot, k] = jnp.broadcast_to(piece, (ext, LANES))
+
+        @pl.when(jnp.logical_not(exists))
+        def _(e=e, at=at):
+            for k in range(per_column):
+                for x in range(2):
+                    xsmall[at, x, k, pl.ds(e * packs, packs)] = jnp.zeros((packs, LANES), jnp.float32)
+
+    for t in range(tiles):
+        drain(recv[t].at[pl.ds(0, (gz_n - 1) * slots), pl.ds(0, width[t])], in_sem.at[tiles + t])
+        for k in range(per_column):
+            block = recv[t][source[k]]
+            xsend[t, 0, k] = block[:nfield, :halo]
+            xsend[t, 1, k] = block[:nfield, rows - halo :]
+            vals[:, t, k, halo : halo + rows, :] = block[:nfield]
+            if t < tiles - 1:
+                piece = block[nfield:]
+                packed[1 + t, k] = piece
+                for x, r in ((0, 0), (1, rows - 1)):
+                    for n in range(packs):
+                        xsmall[t, x, k, pl.ds(packs + n, 1)] = piece[n, r : r + 1]
+
+        for e, (exists, _, device) in enumerate(sides_x):
+
+            @pl.when(exists)
+            def _(t=t, e=e, device=device):
+                for src, dst, sem in ((xsend, xghost, x_sem), (xsmall, xgsmall, xs_sem)):
+                    pltpu.make_async_remote_copy(
+                        src_ref=src.at[t, e],
+                        dst_ref=dst.at[t, 1 - e],
+                        send_sem=sem.at[t, e],
+                        recv_sem=sem.at[t, 2 + 1 - e],
+                        device_id=device,
+                        device_id_type=MESH,
+                    ).start()
+
+            @pl.when(jnp.logical_not(exists))
+            def _(t=t, e=e):
+                for h in range(halo):
+                    xghost[t, e, :, :, h : h + 1, :] = xsend[t, e, :, :, halo - 1 - h : halo - h, :]
+                xgsmall[t, e] = xsmall[t, e]
+
+    near = (halo - 1, halo + rows)
+    first = (0, halo + rows)
+    shape = (per_column, ext, LANES)
+    lane3 = lax.broadcasted_iota(jnp.int32, shape, 2)
+    z_cell = lane3 % cells
+    group = lane3 // cells
+    last_group = LANES // cells - 1
+    row_id = lax.broadcasted_iota(jnp.int32, shape, 1)
+    far = lane3 >= LANES // 2
+
+    def mirror(v, e):
+        ring = None
+        for h in range(halo):
+            shift = (2 * h + 1) * cells
+            w = rolled(v, shift if e else -shift)
+            spot = h if e else last_group - h
+            ring = w if ring is None else jnp.where(group == spot, w, ring)
+        return ring
+
+    def spread(t, e):
+        for n in range(packs):
+            unpack[:, halo : halo + rows, :] = packed[e and 1 + t, :, n]
+            for x in range(2):
+                unpack[:, near[x] : near[x] + 1, :] = xgsmall[t, x, :, pl.ds(e * packs + n, 1), :]
+            whole = unpack[...]
+            for j in range(min(per_pack, nfield - n * per_pack)):
+                shift = -strip_lanes * j if e else -strip_lanes * (j + 1)
+                edge[e and 1 + t, n * per_pack + j] = rolled(whole, shift)
+
+    def shift_rows(v, by):
+        if ext % 8 == 0:
+            return pltpu.roll(v, by % ext, 1)
+        cut = by % ext
+        return jnp.concatenate([v[:, ext - cut :], v[:, : ext - cut]], 1)
+
+    def around(v, below, above):
+        below_y = jnp.where(group == 0, below, rolled(v, cells))
+        above_y = jnp.where(group == last_group, above, rolled(v, -cells))
+        before_k = jnp.concatenate([v[-1:], v[:-1]], 0)
+        after_k = jnp.concatenate([v[1:], v[:1]], 0)
+        below_z = jnp.where(z_cell == 0, rolled(before_k, 1 - cells), rolled(v, 1))
+        above_z = jnp.where(z_cell == cells - 1, rolled(after_k, cells - 1), rolled(v, -1))
+        total = shift_rows(v, 1) + shift_rows(v, -1) + below_y + above_y + below_z + above_z
+        return total - 6.0 * v
+
+    x_cell = row_id + (gx * cells + part * rows - halo)
+    x_cell = jnp.where(x_cell < 0, -1 - x_cell, x_cell)
+    x_end = gx_n * cells
+    x_cell = jnp.where(x_cell > x_end - 1, 2 * x_end - 1 - x_cell, x_cell)
+    xglob = x_cell.astype(jnp.float32)
+    unpack[...] = jnp.zeros_like(unpack)
+
+    for t in range(tiles):
+        for e, (exists, _, device) in enumerate(sides_x):
+
+            @pl.when(exists)
+            def _(t=t, e=e):
+                drain(xghost.at[t, e], x_sem.at[t, 2 + e])
+                drain(xgsmall.at[t, e], xs_sem.at[t, 2 + e])
+
+        for k in range(per_column):
+            for e in range(2):
+                vals[:, t, k, first[e] : first[e] + halo, :] = xghost[t, e, k]
+                marks[t, k, near[e] : near[e] + 1, :] = xgsmall[t, e, k, pl.ds(2 * packs, 1)]
+        for e, (exists, _) in enumerate(sides_y):
+            if e == 0 and t > 0:
+                continue
+            if e == 1 and t < tiles - 1:
+                spread(t, e)
+                continue
+
+            @pl.when(exists)
+            def _(t=t, e=e):
+                spread(t, e)
+
+            @pl.when(jnp.logical_not(exists))
+            def _(t=t, e=e):
+                for f in range(nfield):
+                    edge[e and 1 + t, f] = mirror(vals[f, t], e)
+                edge_marks[e and 1 + t] = mirror(marks[t], e)
+
+        def join(low, high):
+            return jnp.where(far, low, high) if t == 0 else high
+
+        for step in range(STEPS):
+            last = step == STEPS - 1
+            if step == 0:
+                body = [vals[f, t] for f in range(nfield)]
+                rim = [join(edge[0, f], edge[1 + t, f]) for f in range(nfield)]
+                seed = (marks[t], join(edge_marks[0], edge_marks[1 + t]))
+            else:
+                body = [mid[f, t] for f in range(nfield)]
+                rim = [mid_edge[f] for f in range(nfield)]
+
+            def laplace(f):
+                v, w = body[f], rim[f]
+                prior = w if t == 0 else (vals[f, t - 1] if step == 0 else mid[f, t - 1])
+                sums = [around(v, rolled(prior, cells), rolled(w, -cells))]
+                if not last:
+                    sums.append(around(w, rolled(v, cells), rolled(v, -cells)))
+                return sums
+
+            def keep(f, i, new):
+                if last:
+                    result[t, :, f] = new[:, halo : halo + rows]
+                elif i == 0:
+                    mid[f, t] = new
+                else:
+                    mid_edge[f] = new
+
+            thermal = xglob / (2.0 * cells) - 1.0 - 0.25 * step
+            change = []
+            for k in range(NPHASE):
+                moved = []
+                for i, lap in enumerate(laplace(k)):
+                    have = (body, rim)[i]
+                    phi = have[k]
+                    drive = gain[k] * thermal
+                    for j in range(nfield - NPHASE):
+                        drive = drive + couple[k, j] * have[NPHASE + j]
+                    if step == 0:
+                        drive = drive + jnp.where(seed[i] == float(k), SEED_GAIN, 0.0)
+                    delta = 0.12 * lap + phi * (1.0 - phi) * (phi - 0.5 + drive)
+                    moved.append(delta)
+                    keep(k, i, phi + delta)
+                change.append(moved)
+            for j in range(nfield - NPHASE):
+                for i, lap in enumerate(laplace(NPHASE + j)):
+                    new = (body, rim)[i][NPHASE + j] + (0.1 * diffuse[j]) * lap
+                    for k in range(NPHASE):
+                        new = new - latent[j, k] * change[k][i]
+                    keep(NPHASE + j, i, new)
+
+        for p in range(places):
+            k = depth[p]
+            outbuf[t, p // slots, p % slots] = jnp.where(k >= 0, result[t, jnp.maximum(k, 0)], 0.0)
+        for d in range(gz_n - 1, 0, -1):
+            to = (gz + d) % gz_n
+            pltpu.make_async_remote_copy(
+                src_ref=outbuf.at[t, to],
+                dst_ref=outrecv.at[t, part],
+                send_sem=out_sem.at[t],
+                recv_sem=out_sem.at[tiles + t],
+                device_id=(gx, gy, to),
+                device_id_type=MESH,
+            ).start()
+        outrecv[t, part] = outbuf[t, gz]
+
+    for e, (exists, _) in enumerate(sides_y):
+
+        @pl.when(exists)
+        def _(e=e):
+            drain(strip.at[e], strip_sem.at[e])
+            drain(strip_seed[e], strip_seed_sem.at[e])
+
+    drain(seed_recv.at[pl.ds(0, gz_n - 1)], seed_sem.at[0])
+    for t in range(tiles):
+        drain(recv[t].at[pl.ds(0, (gz_n - 1) * slots), pl.ds(0, width[t])], in_sem.at[t])
+        for e, (exists, _, device) in enumerate(sides_x):
+
+            @pl.when(exists)
+            def _(t=t, e=e):
+                drain(xsend.at[t, e], x_sem.at[t, e])
+                drain(xsmall.at[t, e], xs_sem.at[t, e])
+
+    for t in range(tiles):
+        drain(outrecv.at[t, pl.ds(0, gz_n - 1)], out_sem.at[tiles + t])
+        for q in range(gz_n):
+            out[:, :, q * rows : (q + 1) * rows, t * LANES : (t + 1) * LANES] = outrecv[t, q]
+    for t in range(tiles):
+        drain(outbuf.at[t, pl.ds(0, gz_n - 1)], out_sem.at[t])
+
+
 def solution(mesh):
     gx_n, gy_n, gz_n = mesh.shape["gx"], mesh.shape["gy"], mesh.shape["gz"]
+
+    def deep(fields, seeds, *tables):
+        slots, nfield, cells, surface = fields.shape
+        tables = (tables[0].T,) + tables[1:]
+        nblk = tables[0].shape[1]
+        column = nblk // (gx_n * gy_n)
+        tiles = surface // LANES
+        rows = cells // gz_n
+        ext = rows + 2 * STEPS
+        packs = -(-nfield // (LANES // (STEPS * cells)))
+        places = gz_n * slots
+        f32, i32 = jnp.float32, jnp.int32
+        dma = pltpu.SemaphoreType.DMA
+        anyspace = pl.BlockSpec(memory_space=pl.ANY)
+        block = (column, ext, LANES)
+        faces = (tiles, 2, column, nfield, STEPS, LANES)
+        thin = (tiles, 2, column, 2 * packs + 1, LANES)
+        return pl.pallas_call(
+            functools.partial(deep_kernel, (gx_n, gy_n, gz_n, nblk, cells, surface)),
+            out_shape=pltpu.VMEM(fields.shape, f32),
+            in_specs=[anyspace] * 9,
+            out_specs=pl.BlockSpec(memory_space=pltpu.VMEM),
+            scratch_shapes=[pltpu.SMEM(a.shape, a.dtype) for a in tables]
+            + [
+                dma((len(tables),)),
+                pltpu.VMEM(fields.shape, f32),
+                pltpu.VMEM((tiles, gz_n, slots, nfield + packs, rows, LANES), f32),
+                pltpu.VMEM((gz_n, slots, surface), i32),
+                pltpu.VMEM((2, gz_n, slots, packs, rows, LANES), f32),
+                pltpu.VMEM((nfield, tiles) + block, f32),
+                pltpu.VMEM((tiles + 1, nfield) + block, f32),
+                pltpu.VMEM((nfield, tiles) + block, f32),
+                pltpu.VMEM((nfield,) + block, f32),
+                pltpu.VMEM((tiles,) + block, f32),
+                pltpu.VMEM((tiles + 1,) + block, f32),
+                pltpu.VMEM(faces, f32),
+                pltpu.VMEM(faces, f32),
+                pltpu.VMEM(thin, f32),
+                pltpu.VMEM(thin, f32),
+                pltpu.VMEM((tiles + 1, column, packs, rows, LANES), f32),
+                pltpu.VMEM(block, f32),
+                pltpu.VMEM((tiles, column, nfield, rows, LANES), f32),
+                pltpu.VMEM((tiles, gz_n, slots, nfield, rows, LANES), f32),
+                pltpu.VMEM((tiles, gz_n, slots, nfield, rows, LANES), f32),
+                dma((2,)),
+                dma((2 * tiles,)),
+                dma((2,)),
+                dma((4,)),
+                dma((4,)),
+                dma((tiles, 4)),
+                dma((tiles, 4)),
+                dma((2 * tiles,)),
+            ]
+            + [pltpu.VMEM((places, packs, rows, LANES), f32)] * 2
+            + [pltpu.VMEM((gz_n, slots, surface), i32)] * 2
+            + [pltpu.VMEM((places, w, rows, LANES), f32) for w in [nfield + packs] * (tiles - 1) + [nfield]],
+            compiler_params=pltpu.CompilerParams(collective_id=0, has_side_effects=True),
+        )(fields, seeds, *tables)
 
     def per_device(fields, seeds, coords, neighbours, before, after, couple, latent, diffuse, gain):
         slots, nfield, cells, surface = fields.shape
@@ -302,10 +824,12 @@
         dma = pltpu.SemaphoreType.DMA
         smem = pl.BlockSpec(memory_space=pltpu.SMEM)
         anyspace = pl.BlockSpec(memory_space=pl.ANY)
+        if cells % gz_n == 0 and cells // gz_n >= STEPS and 2 * STEPS * cells <= LANES:
+            return deep(fields, seeds, coords, before, after, couple, latent, diffuse, gain)
         faces_x = (STEPS, 2, per_column, nfield, LANES)
         faces_y = (STEPS, 2, per_column, rows, LANES)
         return pl.pallas_call(
-            functools.partial(kernel, (gx_n, gy_n, gz_n, nblk, cells, surface)),
+            functools.partial(tile_kernel, (gx_n, gy_n, gz_n, nblk, cells, surface)),
             out_shape=pltpu.VMEM(fields.shape, f32),
             in_specs=[anyspace, anyspace] + [smem] * 7,
             out_specs=pl.BlockSpec(memory_space=pltpu.VMEM),

time: 28 us -> 25.7 us (0.918)
  Pallas kernels: 27.2 us -> 24.9 us
    pallas_call x1, Pallas kernels: 27.2 us -> 24.9 us  [deep(): pl.pallas_call(functools.partial(deep_kernel, (gx_n, gy_n, gz_n, nblk, ce...]
where the time goes in v2:
time: 25.7 us; the launch traced here: 25.6 us
  Pallas kernels  24.9 us (97%)
  local copies, waits for them, and re-layouts  0.71 us (3%)
    pallas_call x1, Pallas kernels, deep(): pl.pallas_call(functools.partial(deep_kernel, (gx_n, gy_n, gz_n, nblk, ce...  24.9 us
    unnamed x1, local copies, waits for them, and re-layouts  0.71 us

profile of v2, /device:TPU:0, one launch (start us, length us, event | category | flops | bytes accessed | tf_op | source)
XLA Modules:
  0.0 25.6 jit_solution(10554891284201550624)
XLA Ops:
  0.0 24.9 %shard_map.91 = f32[2,8,16,256]{3,2,1,0:T(8,128)S(1)} custom-call(f32[2,8,16,256]{3,2,1,0:T(8,128)} %fields.1, s32[2,256]{1,0:T(2,128)} %seeds.1, s32[3,48]{1,0:T(4,128)} %bitcast.1, s32[48]{0:T(128)} %refs_1_.1, s32[48]{0:T(128)} %refs_2_.1, f32[4,4]{1,0:T(4,128)} %refs_3_.1, f32[4,4]{1,0:T(4,128)} %refs_4_.1, f32[4]{0:T(128)} %refs_5_.1, f32[4]{0:T(128)} %refs_6_.1), custom_call_target="tpu_custom_call" | custom-call | tf_op jit(solution)/shard_map/pallas_call | solution.py:775
  24.9 0.7 %copy.11 = f32[2,8,16,256]{3,2,1,0:T(8,128)} copy(f32[2,8,16,256]{3,2,1,0:T(8,128)S(1)} %shard_map.91) | data formatting | bytes 524288

commit v3 on v2

--- a/solution.py
+++ b/solution.py
@@ -287,6 +287,14 @@
     own.wait()
     for copy in moves:
         copy.wait()
+
+
+def widths(nfield, tiles, cells):
+    per_pack = LANES // (STEPS * cells)
+    packs = -(-nfield // per_pack)
+    fold = per_pack > 1 and nfield % per_pack == 0
+    data = [nfield - packs if fold and t > 0 else nfield for t in range(tiles)]
+    return data, [w + (packs if t < tiles - 1 else 0) for t, w in enumerate(data)]
 
 
 def deep_kernel(sizes, fields, seeds, *refs):
@@ -340,6 +348,7 @@
     per_pack = LANES // strip_lanes
     packs = -(-nfield // per_pack)
     places = gz_n * slots
+    data_width, width = widths(nfield, tiles, cells)
     gx, gy, gz = lax.axis_index("gx"), lax.axis_index("gy"), lax.axis_index("gz")
     odd_x = gx % 2
     turn = 1 - 2 * odd_x
@@ -418,12 +427,22 @@
                     strip[e, q, s, pl.ds(n, 1)] = row
             for t in range(tiles - 1):
                 for q, row in enumerate(pack(s, n, t + 1, 0)):
-                    bulk[t, q, s, pl.ds(nfield + n, 1)] = row
+                    bulk[t, q, s, pl.ds(data_width[t] + n, 1)] = row
+    folds = per_pack - 1
     for t in range(tiles):
-        for q in range(gz_n):
-            bulk[t, q, :, pl.ds(0, nfield)] = mine[
-                :, :, q * rows : (q + 1) * rows, t * LANES : (t + 1) * LANES
-            ]
+        if data_width[t] == nfield:
+            for q in range(gz_n):
+                bulk[t, q, :, pl.ds(0, nfield)] = mine[
+                    :, :, q * rows : (q + 1) * rows, t * LANES : (t + 1) * LANES
+                ]
+            continue
+        for n in range(packs):
+            extra = mine[:, n * per_pack + folds, :, t * LANES : (t + 1) * LANES]
+            for i in range(folds):
+                row = mine[:, n * per_pack + i, :, t * LANES : (t + 1) * LANES]
+                row = jnp.where(lane < strip_lanes, rolled(extra, -strip_lanes * (i + 1)), row)
+                for q in range(gz_n):
+                    bulk[t, q, :, n * folds + i] = row[:, q * rows : (q + 1) * rows]
     pl.semaphore_wait(barrier, expected)
 
     for e, (exists, other) in enumerate(sides_y):
@@ -458,7 +477,6 @@
             device_id_type=MESH,
         ).start()
 
-    width = [nfield + packs] * (tiles - 1) + [nfield]
     for t in range(tiles):
         for d in range(gz_n - 1, 0, -1):
             to = (gz + d) % gz_n
@@ -546,15 +564,38 @@
                 for x in range(2):
                     xsmall[at, x, k, pl.ds(e * packs, packs)] = jnp.zeros((packs, LANES), jnp.float32)
 
+    def unfold(block, strips):
+        fields_of = []
+        for n in range(packs):
+            strip_n = strips[n : n + 1]
+            extra = rolled(strip_n, -strip_lanes * folds)
+            for i in range(folds):
+                row = block[n * folds + i : n * folds + i + 1]
+                fields_of.append(
+                    jnp.where(lane < strip_lanes, rolled(strip_n, -strip_lanes * i), row)
+                )
+                extra = jnp.where(
+                    lane // strip_lanes == i + 1, rolled(row, strip_lanes * (i + 1)), extra
+                )
+            fields_of.append(extra)
+        return fields_of
+
     for t in range(tiles):
         drain(recv[t].at[pl.ds(0, (gz_n - 1) * slots), pl.ds(0, width[t])], in_sem.at[tiles + t])
         for k in range(per_column):
             block = recv[t][source[k]]
-            xsend[t, 0, k] = block[:nfield, :halo]
-            xsend[t, 1, k] = block[:nfield, rows - halo :]
-            vals[:, t, k, halo : halo + rows, :] = block[:nfield]
+            if data_width[t] == nfield:
+                full = block[:nfield]
+                xsend[t, 0, k] = full[:, :halo]
+                xsend[t, 1, k] = full[:, rows - halo :]
+                vals[:, t, k, halo : halo + rows, :] = full
+            else:
+                for f, v in enumerate(unfold(block, packed[t, k])):
+                    xsend[t, 0, k, pl.ds(f, 1)] = v[:, :halo]
+                    xsend[t, 1, k, pl.ds(f, 1)] = v[:, rows - halo :]
+                    vals[pl.ds(f, 1), t, k, halo : halo + rows, :] = v
             if t < tiles - 1:
-                piece = block[nfield:]
+                piece = block[data_width[t] :]
                 packed[1 + t, k] = piece
                 for x, r in ((0, 0), (1, rows - 1)):
                     for n in range(packs):
@@ -810,7 +851,7 @@
             ]
             + [pltpu.VMEM((places, packs, rows, LANES), f32)] * 2
             + [pltpu.VMEM((gz_n, slots, surface), i32)] * 2
-            + [pltpu.VMEM((places, w, rows, LANES), f32) for w in [nfield + packs] * (tiles - 1) + [nfield]],
+            + [pltpu.VMEM((places, w, rows, LANES), f32) for w in widths(nfield, tiles, cells)[1]],
             compiler_params=pltpu.CompilerParams(collective_id=0, has_side_effects=True),
         )(fields, seeds, *tables)
 

time: 25.7 us -> 25.1 us (0.977)
  Pallas kernels: 24.9 us -> 24.3 us
    pallas_call x1, Pallas kernels: 24.9 us -> 24.3 us  [deep(): pl.pallas_call(functools.partial(deep_kernel, (gx_n, gy_n, gz_n, nblk, ce...]
where the time goes in v3:
time: 25.1 us; the launch traced here: 25 us
  Pallas kernels  24.3 us (97%)
  local copies, waits for them, and re-layouts  0.71 us (3%)
    pallas_call x1, Pallas kernels, deep(): pl.pallas_call(functools.partial(deep_kernel, (gx_n, gy_n, gz_n, nblk, ce...  24.3 us
    unnamed x1, local copies, waits for them, and re-layouts  0.71 us

profile of v3, /device:TPU:0, one launch (start us, length us, event | category | flops | bytes accessed | tf_op | source)
XLA Modules:
  0.0 25.0 jit_solution(17386937131560201844)
XLA Ops:
  0.0 24.3 %shard_map.91 = f32[2,8,16,256]{3,2,1,0:T(8,128)S(1)} custom-call(f32[2,8,16,256]{3,2,1,0:T(8,128)} %fields.1, s32[2,256]{1,0:T(2,128)} %seeds.1, s32[3,48]{1,0:T(4,128)} %bitcast.1, s32[48]{0:T(128)} %refs_1_.1, s32[48]{0:T(128)} %refs_2_.1, f32[4,4]{1,0:T(4,128)} %refs_3_.1, f32[4,4]{1,0:T(4,128)} %refs_4_.1, f32[4]{0:T(128)} %refs_5_.1, f32[4]{0:T(128)} %refs_6_.1), custom_call_target="tpu_custom_call" | custom-call | tf_op jit(solution)/shard_map/pallas_call | solution.py:816
  24.3 0.7 %copy.11 = f32[2,8,16,256]{3,2,1,0:T(8,128)} copy(f32[2,8,16,256]{3,2,1,0:T(8,128)S(1)} %shard_map.91) | data formatting | bytes 524288

commit v4 on v3

--- a/solution.py
+++ b/solution.py
@@ -312,7 +312,6 @@
         mine,
         bulk,
         seed_recv,
-        strip,
         vals,
         edge,
         mid,
@@ -325,22 +324,25 @@
         xgsmall,
         packed,
         unpack,
+        ysend,
+        yrecv,
+        ynear,
+        ynear_recv,
         result,
         outbuf,
         outrecv,
         local_sem,
         in_sem,
         seed_sem,
-        strip_sem,
-        strip_seed_sem,
+        y_sem,
+        yn_sem,
         x_sem,
         xs_sem,
         out_sem,
-        *arrivals,
+        *recv,
     ) = refs[:7], refs[7:]
     slots, nfield = mine.shape[0], mine.shape[1]
     tiles = surface // LANES
-    strip_recv, strip_seed, recv = arrivals[:2], arrivals[2:4], arrivals[4:]
     per_column = vals.shape[2]
     rows, halo = cells // gz_n, STEPS
     ext = rows + 2 * halo
@@ -366,7 +368,10 @@
         ins = inside.astype(jnp.int32)
         device = (gx + step_x * (1 - ins), gy, gz + step_x * turn * ins)
         sides_x.append((exists, inside, device))
-    sides_y = ((gy > 0, gy - 1), (gy < gy_n - 1, gy + 1))
+    odd_y = gy % 2
+    sides_y = []
+    for other in (gy - 1 + 2 * odd_y, gy + 1 - 2 * odd_y):
+        sides_y.append((jnp.logical_and(other >= 0, other < gy_n), other))
 
     barrier = pltpu.get_barrier_semaphore()
     expected = gz_n - 1
@@ -374,16 +379,18 @@
         pl.semaphore_signal(
             barrier, inc=1, device_id=(gx, gy, (gz + d) % gz_n), device_id_type=MESH
         )
-    for exists, other in sides_y:
+    targets = [(exists, (gx, other, gz)) for exists, other in sides_y]
+    for exists_x, _, device in sides_x:
+        for exists_y, other in sides_y:
+            both = jnp.logical_and(exists_x, exists_y)
+            targets.append((both, (device[0], other, device[2])))
+    for exists, device in targets:
 
         @pl.when(exists)
-        def _(other=other):
-            for z in range(gz_n):
-                pl.semaphore_signal(
-                    barrier, inc=1, device_id=(gx, other, z), device_id_type=MESH
-                )
-
-        expected = expected + gz_n * exists.astype(jnp.int32)
+        def _(device=device):
+            pl.semaphore_signal(barrier, inc=1, device_id=device, device_id_type=MESH)
+
+        expected = expected + exists.astype(jnp.int32)
     for exists, inside, device in sides_x:
         outside = jnp.logical_and(exists, jnp.logical_not(inside))
 
@@ -411,22 +418,37 @@
         shift = shift % LANES
         return v if shift == 0 else pltpu.roll(v, shift, 2)
 
-    def pack(s, n, t, e):
+    def pack(s, n, t):
         row = None
         for j in range(min(per_pack, nfield - n * per_pack)):
             v = mine[s, pl.ds(n * per_pack + j, 1), :, pl.ds(t * LANES, LANES)]
-            v = rolled(v, strip_lanes * (j + e))
+            v = rolled(v, strip_lanes * j)
             row = v if row is None else jnp.where(lane // strip_lanes == j, v, row)
         return [row[:, q * rows : (q + 1) * rows] for q in range(gz_n)]
 
+    def flipped(v):
+        count, size = LANES // cells, 1
+        while size < count:
+            odd_group = lane // cells // size % 2 == 1
+            v = jnp.where(odd_group, rolled(v, size * cells), rolled(v, -size * cells))
+            size *= 2
+        return v
+
     load.wait()
+
+    @pl.when(odd_y == 1)
+    def _():
+        for s in range(slots):
+            for t in range((tiles + 1) // 2):
+                a, b = pl.ds(t * LANES, LANES), pl.ds((tiles - 1 - t) * LANES, LANES)
+                low, high = flipped(mine[s, :, :, a]), flipped(mine[s, :, :, b])
+                mine[s, :, :, a] = high
+                mine[s, :, :, b] = low
+
     for s in range(slots):
         for n in range(packs):
-            for e, t in ((0, 0), (1, tiles - 1)):
-                for q, row in enumerate(pack(s, n, t, e)):
-                    strip[e, q, s, pl.ds(n, 1)] = row
             for t in range(tiles - 1):
-                for q, row in enumerate(pack(s, n, t + 1, 0)):
+                for q, row in enumerate(pack(s, n, t + 1)):
                     bulk[t, q, s, pl.ds(data_width[t] + n, 1)] = row
     folds = per_pack - 1
     for t in range(tiles):
@@ -445,28 +467,6 @@
                     bulk[t, q, :, n * folds + i] = row[:, q * rows : (q + 1) * rows]
     pl.semaphore_wait(barrier, expected)
 
-    for e, (exists, other) in enumerate(sides_y):
-
-        @pl.when(exists)
-        def _(e=e, other=other):
-            for z in range(gz_n):
-                pltpu.make_async_remote_copy(
-                    src_ref=strip.at[e, tile_of(z)],
-                    dst_ref=strip_recv[1 - e].at[pl.ds(slots * gz, slots)],
-                    send_sem=strip_sem.at[e],
-                    recv_sem=strip_sem.at[2 + 1 - e],
-                    device_id=(gx, other, z),
-                    device_id_type=MESH,
-                ).start()
-                pltpu.make_async_remote_copy(
-                    src_ref=seeds,
-                    dst_ref=strip_seed[1 - e].at[gz],
-                    send_sem=strip_seed_sem.at[e],
-                    recv_sem=strip_seed_sem.at[2 + 1 - e],
-                    device_id=(gx, other, z),
-                    device_id_type=MESH,
-                ).start()
-
     for d in range(1, gz_n):
         pltpu.make_async_remote_copy(
             src_ref=seeds,
@@ -496,23 +496,20 @@
     base = (gx * gy_n + gy) * places
 
     def lookup(b, carry):
-        source, low, high, depth = carry
-        cy, z = coords[1, b], coords[2, b]
-        same = coords[0, b] == gx
-        was, now = before[b] - base, after[b] - base
-        here = jnp.where(jnp.logical_and(same, cy == gy), z, -1)
-        under = jnp.where(jnp.logical_and(same, cy == gy - 1), z, -1)
-        over = jnp.where(jnp.logical_and(same, cy == gy + 1), z, -1)
-        now = jnp.where(here >= 0, now, -1)
-        source = tuple(jnp.where(here == k, was, source[k]) for k in range(per_column))
-        low = tuple(jnp.where(under == k, was + places, low[k]) for k in range(per_column))
-        high = tuple(jnp.where(over == k, was - places, high[k]) for k in range(per_column))
+        source, depth = carry
+        here = jnp.logical_and(coords[0, b] == gx, coords[1, b] == gy)
+        z = jnp.where(here, coords[2, b], -1)
+        was = before[b] - base
+        now = jnp.where(here, after[b] - base, -1)
+        source = tuple(jnp.where(z == k, was, source[k]) for k in range(per_column))
         depth = tuple(jnp.where(now == p, z, depth[p]) for p in range(places))
-        return source, low, high, depth
-
-    none = (jnp.int32(0),) * per_column
-    source, low, high, depth = lax.fori_loop(
-        0, nblk, lookup, (none, none, none, (jnp.int32(-1),) * places)
+        return source, depth
+
+    source, depth = lax.fori_loop(
+        0,
+        nblk,
+        lookup,
+        ((jnp.int32(0),) * per_column, (jnp.int32(-1),) * places),
     )
 
     def drain(ref, sem):
@@ -528,41 +525,18 @@
     load_seed.wait()
     drain(seed_recv.at[pl.ds(0, gz_n - 1)], seed_sem.at[1])
     for k in range(per_column):
-        row = seed_row(seed_recv, source[k])
+        row = seed_row(seed_recv, source[k])[None]
+        cut = [row[:, :, t * LANES : (t + 1) * LANES] for t in range(tiles)]
         for t in range(tiles):
-            piece = row[:, t * LANES : (t + 1) * LANES]
+            piece = jnp.where(odd_y == 1, flipped(cut[tiles - 1 - t]), cut[t])[0]
             wide = jnp.broadcast_to(piece, (ext, LANES))
             marks[t, k] = wide
             if t > 0:
                 edge_marks[t, k] = wide
             for x in range(2):
-                xsmall[t, x, k, pl.ds(2 * packs, 1)] = piece
-                if t > 0:
+                xsmall[t, x, k, pl.ds(packs, 1)] = piece
+                if t == tiles - 1:
                     xsmall[t, x, k, pl.ds(0, packs)] = jnp.zeros((packs, LANES), jnp.float32)
-
-    for e, (exists, _) in enumerate(sides_y):
-        spot, at = (0, 0) if e == 0 else (tiles, tiles - 1)
-
-        @pl.when(exists)
-        def _(e=e, spot=spot, at=at):
-            drain(strip_recv[e], strip_sem.at[2 + e])
-            drain(strip_seed[e], strip_seed_sem.at[2 + e])
-            for k in range(per_column):
-                p = (low, high)[e][k]
-                piece = strip_recv[e][p]
-                packed[spot, k] = piece
-                for x, r in ((0, 0), (1, rows - 1)):
-                    for n in range(packs):
-                        xsmall[at, x, k, pl.ds(e * packs + n, 1)] = piece[n, r : r + 1]
-                row = seed_row(strip_seed[e], p)
-                piece = row[:, surface - LANES :] if e == 0 else row[:, :LANES]
-                edge_marks[spot, k] = jnp.broadcast_to(piece, (ext, LANES))
-
-        @pl.when(jnp.logical_not(exists))
-        def _(e=e, at=at):
-            for k in range(per_column):
-                for x in range(2):
-                    xsmall[at, x, k, pl.ds(e * packs, packs)] = jnp.zeros((packs, LANES), jnp.float32)
 
     def unfold(block, strips):
         fields_of = []
@@ -580,6 +554,74 @@
             fields_of.append(extra)
         return fields_of
 
+    near = (halo - 1, halo + rows)
+    first = (0, halo + rows)
+    shape = (per_column, ext, LANES)
+    lane3 = lax.broadcasted_iota(jnp.int32, shape, 2)
+    z_cell = lane3 % cells
+    group = lane3 // cells
+    last_group = LANES // cells - 1
+    row_id = lax.broadcasted_iota(jnp.int32, shape, 1)
+    far = lane3 >= LANES // 2
+
+    def mirror(v, e):
+        ring = None
+        for h in range(halo):
+            shift = (2 * h + 1) * cells
+            w = rolled(v, shift if e else -shift)
+            spot = h if e else last_group - h
+            ring = w if ring is None else jnp.where(lane // cells == spot, w, ring)
+        return ring
+
+    def outer(t):
+        return [e for e, spot in ((0, 0), (1, tiles - 1)) if t == spot]
+
+    def send_strips(t, e, other):
+        for n in range(packs):
+            row = None
+            for j in range(min(per_pack, nfield - n * per_pack)):
+                v = mirror(vals[n * per_pack + j, t, :, halo : halo + rows, :], e)
+                v = rolled(v, strip_lanes * (j if e else j + 1))
+                row = v if row is None else jnp.where(lane // strip_lanes == j, v, row)
+            ysend[e, :, n] = row
+            for x, r in ((0, 0), (1, rows - 1)):
+                ynear[e, x, :, pl.ds(n, 1), :] = row[:, r : r + 1]
+        ysend[e, :, packs] = mirror(marks[t], e)[:, halo : halo + rows]
+        pltpu.make_async_remote_copy(
+            src_ref=ysend.at[e],
+            dst_ref=yrecv.at[e],
+            send_sem=y_sem.at[e],
+            recv_sem=y_sem.at[2 + e],
+            device_id=(gx, other, gz),
+            device_id_type=MESH,
+        ).start()
+        for x, (exists, _, device) in enumerate(sides_x):
+
+            @pl.when(exists)
+            def _(x=x, device=device):
+                pltpu.make_async_remote_copy(
+                    src_ref=ynear.at[e, x],
+                    dst_ref=ynear_recv.at[e, 1 - x],
+                    send_sem=yn_sem.at[e, x],
+                    recv_sem=yn_sem.at[e, 2 + 1 - x],
+                    device_id=(device[0], other, device[2]),
+                    device_id_type=MESH,
+                ).start()
+
+    def take_strips(e):
+        drain(yrecv.at[e], y_sem.at[2 + e])
+        for x, (exists, _, _) in enumerate(sides_x):
+
+            @pl.when(exists)
+            def _(x=x):
+                drain(ynear_recv.at[e, x], yn_sem.at[e, 2 + x])
+
+            @pl.when(jnp.logical_not(exists))
+            def _(x=x):
+                r = (rows - 1) * x
+                for n in range(packs):
+                    ynear_recv[e, x, :, pl.ds(n, 1), :] = yrecv[e, :, n, r : r + 1, :]
+
     for t in range(tiles):
         drain(recv[t].at[pl.ds(0, (gz_n - 1) * slots), pl.ds(0, width[t])], in_sem.at[tiles + t])
         for k in range(per_column):
@@ -590,16 +632,23 @@
                 xsend[t, 1, k] = full[:, rows - halo :]
                 vals[:, t, k, halo : halo + rows, :] = full
             else:
-                for f, v in enumerate(unfold(block, packed[t, k])):
+                for f, v in enumerate(unfold(block, packed[t - 1, k])):
                     xsend[t, 0, k, pl.ds(f, 1)] = v[:, :halo]
                     xsend[t, 1, k, pl.ds(f, 1)] = v[:, rows - halo :]
                     vals[pl.ds(f, 1), t, k, halo : halo + rows, :] = v
             if t < tiles - 1:
                 piece = block[data_width[t] :]
-                packed[1 + t, k] = piece
+                packed[t, k] = piece
                 for x, r in ((0, 0), (1, rows - 1)):
                     for n in range(packs):
-                        xsmall[t, x, k, pl.ds(packs + n, 1)] = piece[n, r : r + 1]
+                        xsmall[t, x, k, pl.ds(n, 1)] = piece[n, r : r + 1]
+
+        for e in outer(t):
+            exists, other = sides_y[e]
+
+            @pl.when(exists)
+            def _(t=t, e=e, other=other):
+                send_strips(t, e, other)
 
         for e, (exists, _, device) in enumerate(sides_x):
 
@@ -621,30 +670,12 @@
                     xghost[t, e, :, :, h : h + 1, :] = xsend[t, e, :, :, halo - 1 - h : halo - h, :]
                 xgsmall[t, e] = xsmall[t, e]
 
-    near = (halo - 1, halo + rows)
-    first = (0, halo + rows)
-    shape = (per_column, ext, LANES)
-    lane3 = lax.broadcasted_iota(jnp.int32, shape, 2)
-    z_cell = lane3 % cells
-    group = lane3 // cells
-    last_group = LANES // cells - 1
-    row_id = lax.broadcasted_iota(jnp.int32, shape, 1)
-    far = lane3 >= LANES // 2
-
-    def mirror(v, e):
-        ring = None
-        for h in range(halo):
-            shift = (2 * h + 1) * cells
-            w = rolled(v, shift if e else -shift)
-            spot = h if e else last_group - h
-            ring = w if ring is None else jnp.where(group == spot, w, ring)
-        return ring
-
-    def spread(t, e):
+    def spread(t, e, inner):
         for n in range(packs):
-            unpack[:, halo : halo + rows, :] = packed[e and 1 + t, :, n]
+            unpack[:, halo : halo + rows, :] = packed[t, :, n] if inner else yrecv[e, :, n]
             for x in range(2):
-                unpack[:, near[x] : near[x] + 1, :] = xgsmall[t, x, :, pl.ds(e * packs + n, 1), :]
+                row = xgsmall[t, x, :, pl.ds(n, 1), :] if inner else ynear_recv[e, x, :, pl.ds(n, 1), :]
+                unpack[:, near[x] : near[x] + 1, :] = row
             whole = unpack[...]
             for j in range(min(per_pack, nfield - n * per_pack)):
                 shift = -strip_lanes * j if e else -strip_lanes * (j + 1)
@@ -684,23 +715,44 @@
         for k in range(per_column):
             for e in range(2):
                 vals[:, t, k, first[e] : first[e] + halo, :] = xghost[t, e, k]
-                marks[t, k, near[e] : near[e] + 1, :] = xgsmall[t, e, k, pl.ds(2 * packs, 1)]
+                marks[t, k, near[e] : near[e] + 1, :] = xgsmall[t, e, k, pl.ds(packs, 1)]
         for e, (exists, _) in enumerate(sides_y):
             if e == 0 and t > 0:
                 continue
             if e == 1 and t < tiles - 1:
-                spread(t, e)
+                spread(t, e, True)
                 continue
 
             @pl.when(exists)
             def _(t=t, e=e):
-                spread(t, e)
+                take_strips(e)
+                spread(t, e, False)
+                for k in range(per_column):
+                    edge_marks[e and 1 + t, k] = jnp.broadcast_to(
+                        yrecv[e, k, packs, 0:1, :], (ext, LANES)
+                    )
 
             @pl.when(jnp.logical_not(exists))
             def _(t=t, e=e):
                 for f in range(nfield):
                     edge[e and 1 + t, f] = mirror(vals[f, t], e)
                 edge_marks[e and 1 + t] = mirror(marks[t], e)
+
+        def send_back(t, at, count):
+            for p in range(places):
+                k = depth[p]
+                tile = result[t, jnp.maximum(k, 0), pl.ds(at, count)]
+                outbuf[t, p // slots, p % slots, pl.ds(at, count)] = jnp.where(k >= 0, tile, 0.0)
+            for d in range(gz_n - 1, 0, -1):
+                to = (gz + d) % gz_n
+                pltpu.make_async_remote_copy(
+                    src_ref=outbuf.at[t, to, :, pl.ds(at, count)],
+                    dst_ref=outrecv.at[t, part, :, pl.ds(at, count)],
+                    send_sem=out_sem.at[t],
+                    recv_sem=out_sem.at[tiles + t],
+                    device_id=(gx, gy, to),
+                    device_id_type=MESH,
+                ).start()
 
         def join(low, high):
             return jnp.where(far, low, high) if t == 0 else high
@@ -747,6 +799,8 @@
                     moved.append(delta)
                     keep(k, i, phi + delta)
                 change.append(moved)
+            if last:
+                send_back(t, 0, NPHASE)
             for j in range(nfield - NPHASE):
                 for i, lap in enumerate(laplace(NPHASE + j)):
                     new = (body, rim)[i][NPHASE + j] + (0.1 * diffuse[j]) * lap
@@ -754,27 +808,19 @@
                         new = new - latent[j, k] * change[k][i]
                     keep(NPHASE + j, i, new)
 
-        for p in range(places):
-            k = depth[p]
-            outbuf[t, p // slots, p % slots] = jnp.where(k >= 0, result[t, jnp.maximum(k, 0)], 0.0)
-        for d in range(gz_n - 1, 0, -1):
-            to = (gz + d) % gz_n
-            pltpu.make_async_remote_copy(
-                src_ref=outbuf.at[t, to],
-                dst_ref=outrecv.at[t, part],
-                send_sem=out_sem.at[t],
-                recv_sem=out_sem.at[tiles + t],
-                device_id=(gx, gy, to),
-                device_id_type=MESH,
-            ).start()
+        send_back(t, NPHASE, nfield - NPHASE)
         outrecv[t, part] = outbuf[t, gz]
 
     for e, (exists, _) in enumerate(sides_y):
 
         @pl.when(exists)
         def _(e=e):
-            drain(strip.at[e], strip_sem.at[e])
-            drain(strip_seed[e], strip_seed_sem.at[e])
+            drain(ysend.at[e], y_sem.at[e])
+            for x, (exists_x, _, _) in enumerate(sides_x):
+
+                @pl.when(exists_x)
+                def _(x=x):
+                    drain(ynear.at[e, x], yn_sem.at[e, x])
 
     drain(seed_recv.at[pl.ds(0, gz_n - 1)], seed_sem.at[0])
     for t in range(tiles):
@@ -788,8 +834,19 @@
 
     for t in range(tiles):
         drain(outrecv.at[t, pl.ds(0, gz_n - 1)], out_sem.at[tiles + t])
-        for q in range(gz_n):
-            out[:, :, q * rows : (q + 1) * rows, t * LANES : (t + 1) * LANES] = outrecv[t, q]
+
+        @pl.when(odd_y == 0)
+        def _(t=t):
+            for q in range(gz_n):
+                out[:, :, q * rows : (q + 1) * rows, t * LANES : (t + 1) * LANES] = outrecv[t, q]
+
+        @pl.when(odd_y == 1)
+        def _(t=t):
+            lanes = pl.ds((tiles - 1 - t) * LANES, LANES)
+            for q in range(gz_n):
+                for s in range(slots):
+                    out[s, :, q * rows : (q + 1) * rows, lanes] = flipped(outrecv[t, q, s])
+
     for t in range(tiles):
         drain(outbuf.at[t, pl.ds(0, gz_n - 1)], out_sem.at[t])
 
@@ -812,7 +869,7 @@
         anyspace = pl.BlockSpec(memory_space=pl.ANY)
         block = (column, ext, LANES)
         faces = (tiles, 2, column, nfield, STEPS, LANES)
-        thin = (tiles, 2, column, 2 * packs + 1, LANES)
+        thin = (tiles, 2, column, packs + 1, LANES)
         return pl.pallas_call(
             functools.partial(deep_kernel, (gx_n, gy_n, gz_n, nblk, cells, surface)),
             out_shape=pltpu.VMEM(fields.shape, f32),
@@ -824,7 +881,6 @@
                 pltpu.VMEM(fields.shape, f32),
                 pltpu.VMEM((tiles, gz_n, slots, nfield + packs, rows, LANES), f32),
                 pltpu.VMEM((gz_n, slots, surface), i32),
-                pltpu.VMEM((2, gz_n, slots, packs, rows, LANES), f32),
                 pltpu.VMEM((nfield, tiles) + block, f32),
                 pltpu.VMEM((tiles + 1, nfield) + block, f32),
                 pltpu.VMEM((nfield, tiles) + block, f32),
@@ -835,8 +891,12 @@
                 pltpu.VMEM(faces, f32),
                 pltpu.VMEM(thin, f32),
                 pltpu.VMEM(thin, f32),
-                pltpu.VMEM((tiles + 1, column, packs, rows, LANES), f32),
+                pltpu.VMEM((max(tiles - 1, 1), column, packs, rows, LANES), f32),
                 pltpu.VMEM(block, f32),
+                pltpu.VMEM((2, column, packs + 1, rows, LANES), f32),
+                pltpu.VMEM((2, column, packs + 1, rows, LANES), f32),
+                pltpu.VMEM((2, 2, column, packs, LANES), f32),
+                pltpu.VMEM((2, 2, column, packs, LANES), f32),
                 pltpu.VMEM((tiles, column, nfield, rows, LANES), f32),
                 pltpu.VMEM((tiles, gz_n, slots, nfield, rows, LANES), f32),
                 pltpu.VMEM((tiles, gz_n, slots, nfield, rows, LANES), f32),
@@ -844,13 +904,11 @@
                 dma((2 * tiles,)),
                 dma((2,)),
                 dma((4,)),
-                dma((4,)),
+                dma((2, 4)),
                 dma((tiles, 4)),
                 dma((tiles, 4)),
                 dma((2 * tiles,)),
             ]
-            + [pltpu.VMEM((places, packs, rows, LANES), f32)] * 2
-            + [pltpu.VMEM((gz_n, slots, surface), i32)] * 2
             + [pltpu.VMEM((places, w, rows, LANES), f32) for w in widths(nfield, tiles, cells)[1]],
             compiler_params=pltpu.CompilerParams(collective_id=0, has_side_effects=True),
         )(fields, seeds, *tables)

time: 25.1 us -> 24.5 us (0.976)
  Pallas kernels: 24.3 us -> 23.7 us
    pallas_call x1, Pallas kernels: 24.3 us -> 23.7 us  [deep(): pl.pallas_call(functools.partial(deep_kernel, (gx_n, gy_n, gz_n, nblk, ce...]
where the time goes in v4:
time: 24.5 us; the launch traced here: 24.4 us
  Pallas kernels  23.7 us (97%)
  local copies, waits for them, and re-layouts  0.71 us (3%)
    pallas_call x1, Pallas kernels, deep(): pl.pallas_call(functools.partial(deep_kernel, (gx_n, gy_n, gz_n, nblk, ce...  23.7 us
    unnamed x1, local copies, waits for them, and re-layouts  0.71 us

profile of v4, /device:TPU:0, one launch (start us, length us, event | category | flops | bytes accessed | tf_op | source)
XLA Modules:
  0.0 24.4 jit_solution(2191821341858311459)
XLA Ops:
  0.0 23.7 %shard_map.91 = f32[2,8,16,256]{3,2,1,0:T(8,128)S(1)} custom-call(f32[2,8,16,256]{3,2,1,0:T(8,128)} %fields.1, s32[2,256]{1,0:T(2,128)} %seeds.1, s32[3,48]{1,0:T(4,128)} %bitcast.1, s32[48]{0:T(128)} %refs_1_.1, s32[48]{0:T(128)} %refs_2_.1, f32[4,4]{1,0:T(4,128)} %refs_3_.1, f32[4,4]{1,0:T(4,128)} %refs_4_.1, f32[4]{0:T(128)} %refs_5_.1, f32[4]{0:T(128)} %refs_6_.1), custom_call_target="tpu_custom_call" | custom-call | tf_op jit(solution)/shard_map/pallas_call | solution.py:873
  23.7 0.7 %copy.11 = f32[2,8,16,256]{3,2,1,0:T(8,128)} copy(f32[2,8,16,256]{3,2,1,0:T(8,128)S(1)} %shard_map.91) | data formatting | bytes 524288

commit v5 on v4

--- a/solution.py
+++ b/solution.py
@@ -738,13 +738,15 @@
                     edge[e and 1 + t, f] = mirror(vals[f, t], e)
                 edge_marks[e and 1 + t] = mirror(marks[t], e)
 
-        def send_back(t, at, count):
+        def collect(t, at, count):
             for p in range(places):
                 k = depth[p]
                 tile = result[t, jnp.maximum(k, 0), pl.ds(at, count)]
                 outbuf[t, p // slots, p % slots, pl.ds(at, count)] = jnp.where(k >= 0, tile, 0.0)
-            for d in range(gz_n - 1, 0, -1):
-                to = (gz + d) % gz_n
+
+        def send_back(t, at, count, order):
+            for n in order:
+                to = n + (gz <= n).astype(jnp.int32)
                 pltpu.make_async_remote_copy(
                     src_ref=outbuf.at[t, to, :, pl.ds(at, count)],
                     dst_ref=outrecv.at[t, part, :, pl.ds(at, count)],
@@ -800,7 +802,8 @@
                     keep(k, i, phi + delta)
                 change.append(moved)
             if last:
-                send_back(t, 0, NPHASE)
+                collect(t, 0, NPHASE)
+                send_back(t, 0, NPHASE, range(gz_n - 1) if t < tiles - 1 else [0])
             for j in range(nfield - NPHASE):
                 for i, lap in enumerate(laplace(NPHASE + j)):
                     new = (body, rim)[i][NPHASE + j] + (0.1 * diffuse[j]) * lap
@@ -808,7 +811,10 @@
                         new = new - latent[j, k] * change[k][i]
                     keep(NPHASE + j, i, new)
 
-        send_back(t, NPHASE, nfield - NPHASE)
+        collect(t, NPHASE, nfield - NPHASE)
+        early = range(gz_n - 1) if t < tiles - 1 else [0]
+        send_back(t, NPHASE, nfield - NPHASE, early)
+        send_back(t, 0, nfield, [n for n in range(gz_n - 1) if n not in early])
         outrecv[t, part] = outbuf[t, gz]
 
     for e, (exists, _) in enumerate(sides_y):

time: 24.5 us -> 23.8 us (0.971)
  Pallas kernels: 23.7 us -> 22.9 us
    pallas_call x1, Pallas kernels: 23.7 us -> 22.9 us  [deep(): pl.pallas_call(functools.partial(deep_kernel, (gx_n, gy_n, gz_n, nblk, ce...]
where the time goes in v5:
time: 23.8 us; the launch traced here: 23.6 us
  Pallas kernels  22.9 us (96%)
  local copies, waits for them, and re-layouts  0.71 us (3%)
    pallas_call x1, Pallas kernels, deep(): pl.pallas_call(functools.partial(deep_kernel, (gx_n, gy_n, gz_n, nblk, ce...  22.9 us
    unnamed x1, local copies, waits for them, and re-layouts  0.71 us

profile of v5, /device:TPU:0, one launch (start us, length us, event | category | flops | bytes accessed | tf_op | source)
XLA Modules:
  0.0 23.6 jit_solution(2036308896390176218)
XLA Ops:
  0.0 22.9 %shard_map.91 = f32[2,8,16,256]{3,2,1,0:T(8,128)S(1)} custom-call(f32[2,8,16,256]{3,2,1,0:T(8,128)} %fields.1, s32[2,256]{1,0:T(2,128)} %seeds.1, s32[3,48]{1,0:T(4,128)} %bitcast.1, s32[48]{0:T(128)} %refs_1_.1, s32[48]{0:T(128)} %refs_2_.1, f32[4,4]{1,0:T(4,128)} %refs_3_.1, f32[4,4]{1,0:T(4,128)} %refs_4_.1, f32[4]{0:T(128)} %refs_5_.1, f32[4]{0:T(128)} %refs_6_.1), custom_call_target="tpu_custom_call" | custom-call | tf_op jit(solution)/shard_map/pallas_call | solution.py:879
  22.9 0.7 %copy.11 = f32[2,8,16,256]{3,2,1,0:T(8,128)} copy(f32[2,8,16,256]{3,2,1,0:T(8,128)S(1)} %shard_map.91) | data formatting | bytes 524288

commit v6 on v5

--- a/solution.py
+++ b/solution.py
@@ -746,7 +746,7 @@
 
         def send_back(t, at, count, order):
             for n in order:
-                to = n + (gz <= n).astype(jnp.int32)
+                to = jnp.where(n < gz, n, gz_n - 1 - n + gz)
                 pltpu.make_async_remote_copy(
                     src_ref=outbuf.at[t, to, :, pl.ds(at, count)],
                     dst_ref=outrecv.at[t, part, :, pl.ds(at, count)],

time: 23.8 us -> 23.8 us (level)
  no operation moved by 1% of the time
where the time goes in v6:
time: 23.8 us; the launch traced here: 23.6 us
  Pallas kernels  22.9 us (96%)
  local copies, waits for them, and re-layouts  0.71 us (3%)
    pallas_call x1, Pallas kernels, deep(): pl.pallas_call(functools.partial(deep_kernel, (gx_n, gy_n, gz_n, nblk, ce...  22.9 us
    unnamed x1, local copies, waits for them, and re-layouts  0.71 us

profile of v6, /device:TPU:0, one launch (start us, length us, event | category | flops | bytes accessed | tf_op | source)
XLA Modules:
  0.0 23.6 jit_solution(11285875866864933604)
XLA Ops:
  0.0 22.9 %shard_map.91 = f32[2,8,16,256]{3,2,1,0:T(8,128)S(1)} custom-call(f32[2,8,16,256]{3,2,1,0:T(8,128)} %fields.1, s32[2,256]{1,0:T(2,128)} %seeds.1, s32[3,48]{1,0:T(4,128)} %bitcast.1, s32[48]{0:T(128)} %refs_1_.1, s32[48]{0:T(128)} %refs_2_.1, f32[4,4]{1,0:T(4,128)} %refs_3_.1, f32[4,4]{1,0:T(4,128)} %refs_4_.1, f32[4]{0:T(128)} %refs_5_.1, f32[4]{0:T(128)} %refs_6_.1), custom_call_target="tpu_custom_call" | custom-call | tf_op jit(solution)/shard_map/pallas_call | solution.py:879
  22.9 0.7 %copy.11 = f32[2,8,16,256]{3,2,1,0:T(8,128)} copy(f32[2,8,16,256]{3,2,1,0:T(8,128)S(1)} %shard_map.91) | data formatting | bytes 524288

commit v7 on v6

--- a/solution.py
+++ b/solution.py
@@ -586,15 +586,6 @@
             ysend[e, :, n] = row
             for x, r in ((0, 0), (1, rows - 1)):
                 ynear[e, x, :, pl.ds(n, 1), :] = row[:, r : r + 1]
-        ysend[e, :, packs] = mirror(marks[t], e)[:, halo : halo + rows]
-        pltpu.make_async_remote_copy(
-            src_ref=ysend.at[e],
-            dst_ref=yrecv.at[e],
-            send_sem=y_sem.at[e],
-            recv_sem=y_sem.at[2 + e],
-            device_id=(gx, other, gz),
-            device_id_type=MESH,
-        ).start()
         for x, (exists, _, device) in enumerate(sides_x):
 
             @pl.when(exists)
@@ -607,6 +598,16 @@
                     device_id=(device[0], other, device[2]),
                     device_id_type=MESH,
                 ).start()
+
+        ysend[e, :, packs] = mirror(marks[t], e)[:, halo : halo + rows]
+        pltpu.make_async_remote_copy(
+            src_ref=ysend.at[e],
+            dst_ref=yrecv.at[e],
+            send_sem=y_sem.at[e],
+            recv_sem=y_sem.at[2 + e],
+            device_id=(gx, other, gz),
+            device_id_type=MESH,
+        ).start()
 
     def take_strips(e):
         drain(yrecv.at[e], y_sem.at[2 + e])
@@ -633,8 +634,6 @@
                 vals[:, t, k, halo : halo + rows, :] = full
             else:
                 for f, v in enumerate(unfold(block, packed[t - 1, k])):
-                    xsend[t, 0, k, pl.ds(f, 1)] = v[:, :halo]
-                    xsend[t, 1, k, pl.ds(f, 1)] = v[:, rows - halo :]
                     vals[pl.ds(f, 1), t, k, halo : halo + rows, :] = v
             if t < tiles - 1:
                 piece = block[data_width[t] :]
@@ -650,6 +649,10 @@
             def _(t=t, e=e, other=other):
                 send_strips(t, e, other)
 
+        if data_width[t] < nfield:
+            for k in range(per_column):
+                xsend[t, 0, k] = vals[:, t, k, halo : 2 * halo, :]
+                xsend[t, 1, k] = vals[:, t, k, rows : rows + halo, :]
         for e, (exists, _, device) in enumerate(sides_x):
 
             @pl.when(exists)

time: 23.8 us -> 23.8 us (level)
  no operation moved by 1% of the time
where the time goes in v7:
time: 23.8 us; the launch traced here: 23.6 us
  Pallas kernels  22.9 us (96%)
  local copies, waits for them, and re-layouts  0.71 us (3%)
    pallas_call x1, Pallas kernels, deep(): pl.pallas_call(functools.partial(deep_kernel, (gx_n, gy_n, gz_n, nblk, ce...  22.9 us
    unnamed x1, local copies, waits for them, and re-layouts  0.71 us

profile of v7, /device:TPU:0, one launch (start us, length us, event | category | flops | bytes accessed | tf_op | source)
XLA Modules:
  0.0 23.6 jit_solution(16869272872289966695)
XLA Ops:
  0.0 22.9 %shard_map.91 = f32[2,8,16,256]{3,2,1,0:T(8,128)S(1)} custom-call(f32[2,8,16,256]{3,2,1,0:T(8,128)} %fields.1, s32[2,256]{1,0:T(2,128)} %seeds.1, s32[3,48]{1,0:T(4,128)} %bitcast.1, s32[48]{0:T(128)} %refs_1_.1, s32[48]{0:T(128)} %refs_2_.1, f32[4,4]{1,0:T(4,128)} %refs_3_.1, f32[4,4]{1,0:T(4,128)} %refs_4_.1, f32[4]{0:T(128)} %refs_5_.1, f32[4]{0:T(128)} %refs_6_.1), custom_call_target="tpu_custom_call" | custom-call | tf_op jit(solution)/shard_map/pallas_call | solution.py:882
  22.9 0.7 %copy.11 = f32[2,8,16,256]{3,2,1,0:T(8,128)} copy(f32[2,8,16,256]{3,2,1,0:T(8,128)S(1)} %shard_map.91) | data formatting | bytes 524288
